TPU v7x, 128 devices: a whole 4x4x4 slice. The times are simulated.
128 devices in a mesh: wide: 16 (over y_hi, z, core), narrow: 8 (over y_lo, x).
Axes of the slice: x: 4, y: 4 (y_hi: 2, y_lo: 2; y = y_hi * 2 + y_lo), z: 4, core: 2. Of those that a mesh axis runs over, the one named last changes fastest.
Arguments:
- inputs: bfloat16 [1, 4096, 4096], P(None, 'narrow', 'wide'), may hold values from -6 to 6
- out_cotangent: bfloat16 [1, 1, 4096, 14336], P(None, None, ('wide', 'narrow')), may hold values from -0.0014648438 to 0.0014648438
- sign_bits: int32 [1, 4096, 16384], P(None, 'wide', 'narrow'), may hold values 0 or 1
- row_pick: int32 [1, 8192], replicated, may hold values from 0 to 4095
- col_pick: int32 [1, 8192], replicated, may hold values from 0 to 16383
Outputs:
- sketch: float32 [1, 1, 8192], P(None, None, ('wide', 'narrow'))
All inputs are finite; a program needn't handle non-finite values. No bound on the sum of `sign_bits` on one device may be relied on, other than what follows from the above.
Results may differ from a plain program's by a relative error of at most 0.0003.
Values may be sent and summed in bfloat16 or wider, within the bound.
A program may use at most 128 MiB of HBM per device.

v0:
```python
import jax
import jax.numpy as jnp
from jax import lax
from jax.sharding import PartitionSpec as P


def hadamard(length):
    index = jnp.arange(length, dtype=jnp.int32)
    parity = jnp.zeros((length, length), jnp.int32)
    for bit_number in range(length.bit_length() - 1):
        parity = parity ^ index[:, None] >> bit_number & 1 & (index[None, :] >> bit_number & 1)
    return (1 - 2 * parity).astype(jnp.float32)


def transform_last(block):
    width_all = block.shape[-1]
    leading = block.ndim - 1
    factors = []
    remain = width_all
    while remain > 1:
        factor = min(128, remain)
        factors.append(factor)
        remain = remain // factor
    shaped = block.reshape(block.shape[:-1] + tuple(factors))
    for placed, factor in enumerate(factors):
        mixed = jnp.tensordot(
            shaped,
            hadamard(factor),
            axes=([leading + placed], [0]),
            precision=lax.Precision.HIGHEST,
        )
        shaped = jnp.moveaxis(mixed, -1, leading + placed)
    return shaped.reshape(block.shape)


def body(inputs, out_cotangent, sign_bits, row_pick, col_pick):
    wide_count = lax.axis_size("wide")
    narrow_count = lax.axis_size("narrow")
    row_local = inputs.shape[2]
    col_local = sign_bits.shape[2]
    hidden_all = out_cotangent.shape[3]
    padded_width = col_local * narrow_count
    whole_inputs = lax.all_gather(inputs, "narrow", axis=1, tiled=True)
    padded_cot = jnp.pad(out_cotangent, ((0, 0), (0, 0), (0, 0), (0, padded_width - hidden_all)))
    column_cot = lax.all_to_all(padded_cot, "narrow", split_axis=3, concat_axis=2, tiled=True)
    grads = jnp.einsum(
        "etr,metc->merc",
        whole_inputs,
        lax.all_gather(column_cot, "wide", axis=2, tiled=True),
        preferred_element_type=jnp.float32,
    )
    signs = (2 * sign_bits - 1).astype(jnp.float32)
    row_mix = hadamard(row_local)
    wide_index = lax.axis_index("wide")
    narrow_index = lax.axis_index("narrow")
    row_high = row_pick // row_local
    row_low = row_pick % row_local
    col_high = col_pick // col_local
    col_low = col_pick % col_local
    position = row_low * col_local + col_low
    block_len = row_local * col_local
    piece_len = block_len // (wide_count * narrow_count)
    signed = grads[:, 0] * signs
    rows_done = jnp.einsum("ij,mjc->mic", row_mix, signed, precision=lax.Precision.HIGHEST)
    local_done = transform_last(rows_done).reshape(signed.shape[0], block_len)
    pieces = local_done.reshape(signed.shape[0], wide_count * narrow_count, piece_len)
    received = lax.all_to_all(pieces, ("wide", "narrow"), split_axis=1, concat_axis=1, tiled=True)
    finished = jnp.einsum(
        "ts,msj->mtj",
        hadamard(wide_count * narrow_count),
        received,
        precision=lax.Precision.HIGHEST,
    )
    my_piece = wide_index * narrow_count + narrow_index
    target = row_high * narrow_count + col_high
    owned = position // piece_len == my_piece
    lookup = target * piece_len + position % piece_len
    picked = jnp.take_along_axis(finished.reshape(signed.shape[0], -1), lookup, axis=1)
    contributions = [jnp.where(owned, picked, jnp.float32(0.0))]
    stacked = jnp.stack(contributions)
    summed = lax.psum_scatter(stacked, ("wide", "narrow"), scatter_dimension=2, tiled=True)
    return summed / jnp.sqrt(jnp.float32(row_pick.shape[1]))


def solution(mesh):
    return jax.shard_map(
        body,
        mesh=mesh,
        in_specs=(
            P(None, "narrow", "wide"),
            P(None, None, ("wide", "narrow"), None),
            P(None, "wide", "narrow"),
            P(),
            P(),
        ),
        out_specs=P(None, None, ("wide", "narrow")),
        check_vma=False,
    )
```

profile of v0, /device:TPU:0, one launch (start us, length us, event | category | flops | bytes accessed | tf_op | source)
XLA Modules:
  0.0 1106.3 jit_solution(14091993724530731446)
XLA Ops:
  6.5 0.7 all-gather.5.cloned.1.call-update
  7.3 14.3 %copy.20 = bf16[1,1,32,14336]{2,1,0,3:T(2,128)(2,1)} copy(bf16[1,1,32,14336]{3,2,1,0:T(8,128)(2,1)} %param.6) | data formatting | bytes 1835008 | tf_op args[1]
  21.6 18.6 %pad_bitcast_fusion = bf16[16384,1,1,32]{3,2,1,0:T(2,128)(2,1)} fusion(bf16[1,1,32,14336]{2,1,0,3:T(2,128)(2,1)} %copy.20), kind=kLoop, calls=%fused_computation.160 | loop fusion | bytes 1966080
  40.2 0.5 broadcast.581
  40.7 90.8 %reduce = bf16[16384,32]{1,0:T(8,128)(2,1)} reduce(bf16[16384,1,1,32]{3,2,1,0:T(2,128)(2,1)} %pad_bitcast_fusion, bf16[]{:T(256)} %broadcast.581), dimensions={1,2}, to_apply=%pad_bitcast_fusion.reduce_sub_computation | reduce | bytes 2097154
  131.5 7.0 reshape.337
  138.4 20.9 %all_to_all.23 = bf16[8,2,32768]{2,1,0:T(2,128)(2,1)S(1)} all-to-all(bf16[8,2,32768]{2,1,0:T(2,128)(2,1)S(1)} %reshape.337), channel_id=1, replica_groups=mesh['wide'=16,'narrow'=8] {'narrow'}, dimensions={0} | all-to-all | bytes 2097152 | tf_op jit(solution)/shard_map/all_to_all | solution.py:45
  159.4 6.2 reshape.338
  165.6 15.1 %copy.21 = bf16[1,1,32,16384]{3,2,1,0:T(8,128)(2,1)S(1)} copy(bf16[1,1,32,16384]{2,1,0,3:T(2,128)(2,1)} %bitcast.73) | data formatting | bytes 2097152 | tf_op jit(solution)/shard_map/all_to_all | solution.py:45
  180.7 0.6 copy.33
  181.3 1.6 copy.22
  182.9 0.1 copy-done
  183.0 2.0 copy.23
  185.1 107.1 %all-gather.3.cloned.1.call-done = bf16[1,1,4096,2048]{3,2,1,0:T(8,128)(2,1)} async-done(((bf16[1,1,256,2048]{3,2,1,0:T(8,128)(2,1)}), bf16[1,1,4096,2048]{3,2,1,0:T(8,128)(2,1)}) %all-gather.3.cloned.1.call-update) | async-done | bytes 16777232 | tf_op jit(solution)/shard_map/all_gather | solution.py:49
  292.2 12.4 %fusion.8 = f32[256,2048]{0,1:T(8,128)S(1)} fusion(bf16[1,1,4096,2048]{3,2,1,0:T(8,128)(2,1)} %all-gather.3.cloned.1.call-done, bf16[1,4096,256]{2,1,0:T(8,128)(2,1)} %all-gather.5.cloned.1.call-done, s32[1,256,2048]{1,2,0:T(8,128)} %copy.23), kind=kOutput, calls=%fused_computation.6 | convolution fusion | flops 4297064448 | bytes 23068672 | tf_op jit(solution)/shard_map/etr,metc->merc/dot_general | solution.py:46
  304.6 2.2 fusion.21
  306.8 4.4 fusion.18
  311.2 29.0 %fusion.14 = f32[256,128,16]{2,1,0:T(8,128)} fusion(f32[256,128,16]{1,0,2:T(8,128)S(1)} %fusion.18, s32[16]{0:T(128)S(1)} %get-tuple-element.21, s32[16]{0:T(128)S(1)} %get-tuple-element.22, s32[16]{0:T(128)S(1)} %get-tuple-element.23, s32[16]{0:T(128)S(1)} %get-tuple-element.24), kind=kOutput, calls=%fused_computation.10 | convolution fusion | flops 100665856 | bytes 4194560 | tf_op jit(solution)/shard_map/dot_general | solution.py:26
  340.2 12.3 %reshape_reshape_reshape.4 = f32[1,128,4096]{2,0,1:T(1,128)} reshape(f32[256,128,16]{2,1,0:T(8,128)} %fusion.14) | data formatting | bytes 4194304 | tf_op jit(solution)/shard_map/reshape;reshape;reshape | solution.py:66
  352.5 6.2 all-to-all-start.1
  358.8 0.3 reduce-scatter.4.cloned.1.call-start
  359.1 0.6 compare_select_fusion
  359.8 28.9 %all-to-all-done.1 = f32[1,128,4096]{2,0,1:T(1,128)S(1)} async-done(((f32[1,128,4096]{2,0,1:T(1,128)}), f32[1,128,4096]{2,0,1:T(1,128)S(1)}, u32[]{:S(2)}, u32[]{:S(2)}) %all-to-all-start.1) | async-done | bytes 2097184 | tf_op jit(solution)/shard_map/all_to_all | solution.py:67
  388.7 5.7 convolution_bitcast_fusion
  394.4 2.9 copy.28
  397.3 2.0 copy.34
  399.3 45.5 %gather_fusion = f32[8192]{0:T(1024)S(1)} fusion(f32[524288]{0:T(1024)S(1)} %bitcast.72, s32[8192]{0:T(1024)S(1)} %broadcast_clamp_fusion), kind=kCustom, calls=%fused_computation | custom fusion | bytes 98304 | tf_op jit(solution)/shard_map/jit(take_along_axis)/gather | solution.py:78
  444.8 0.2 fusion.64
  445.0 6.3 copy.30
  451.4 646.6 %reduce-scatter.4.cloned.1.call-done = f32[64,1]{1,0:T(8,128)} async-done(((f32[8192,1]{1,0:T(8,128)}), f32[64,1]{1,0:T(8,128)}) %reduce-scatter.4.cloned.1.call-update) | async-done | bytes 272
  1098.0 0.8 copy.31
  1098.9 0.5 broadcast_multiply_fusion
  (21 shorter events, 0.2 us)
Async XLA Ops:
  6.5 178.6 %all-gather.5.cloned.1.call-start = ((), (), s32[]{:S(2)}) async-start(), calls=%async_computation.4 | async-start | bytes 2359296 | tf_op jit(solution)/shard_map/all_gather | solution.py:43
  7.3 284.9 %all-gather.3.cloned.1.call-start = ((), (), s32[]{:S(2)}) async-start(), calls=%async_computation.3 | async-start | bytes 17825792 | tf_op jit(solution)/shard_map/all_gather | solution.py:49
  181.3 1.7 copy-start
  352.5 6.6 copy-start.1
  352.5 6.6 copy-start.2
  352.5 36.2 %all-to-all-start.1 = ((f32[1,128,4096]{2,0,1:T(1,128)}), f32[1,128,4096]{2,0,1:T(1,128)S(1)}, u32[]{:S(2)}, u32[]{:S(2)}) async-start(f32[1,128,4096]{2,0,1:T(1,128)} %reshape_reshape_reshape.4), calls=%async_computation.1 | async-start | bytes 4194304 | tf_op jit(solution)/shard_map/all_to_all | solution.py:67
  358.8 739.2 %reduce-scatter.4.cloned.1.call-start = ((), (), s32[]{:S(2)}) async-start(), calls=%async_computation.5 | async-start | bytes 4227072
Sparse Core Ops, SparseCore 0:
  9.0 43.6 all-gather.4
  183.0 109.0 all-gather.2
  451.5 646.4 reduce-scatter.3
where the time goes:
time: 1120 us; the launch traced here: 1110 us
  waiting for transfers between devices  783 us (70%)
  local copies, waits for them, and re-layouts  136 us (12%)
  other arithmetic  92.2 us (8%)
  matrix products  53.7 us (5%)
  blocking collectives  20.9 us (2%)
  between operations  13.7 us (1%)
    unnamed x4, waiting for transfers between devices  647 us
    all_gather x1, waiting for transfers between devices, body(): lax.all_gather(column_cot, 'wide', axis=2, tiled=True)  107 us
    unnamed x1, other arithmetic  90.8 us
    unnamed x16, local copies, waits for them, and re-layouts  58.4 us
    gather x1, local copies, waits for them, and re-layouts, body(): jnp.take_along_axis(finished.reshape(signed.shape[0], -1), lookup, axis=1)  45.5 us
    dot_general x2, matrix products, transform_last(): jnp.tensordot(shaped, hadamard(factor), axes=([leading + placed], [0]), p...  33.4 us
    all_to_all x1, waiting for transfers between devices, body(): lax.all_to_all(pieces, ('wide', 'narrow'), split_axis=1, concat_axis=1, t...  28.9 us
  transfers between devices with their start and end apart: 4, of which 3 were waited for; matrix products, arithmetic and copies ran while one was open for 14% of the time, Pallas kernels for 0%

commit v1 on v0

v1 whole, which is shorter than its diff:
```python
import functools

import jax
import jax.numpy as jnp
from jax import lax
from jax.experimental import pallas as pl
from jax.experimental.pallas import tpu as pltpu
from jax.sharding import PartitionSpec as P

MESH = pl.DeviceIdType.MESH
F32 = jnp.float32
BF16 = jnp.bfloat16
I32 = jnp.int32
VMEM_LIMIT = 60 << 20

TOK = 32
COLS = 2048
ROWS = 256
LAST = 7


def place():
    wide = lax.axis_index("wide")
    narrow = lax.axis_index("narrow")
    return wide, narrow, wide // 8, (wide // 2) % 4, wide % 2, narrow // 4, narrow % 4


def device(y_hi, z, core, y_lo, x):
    return (y_hi * 8 + z * 2 + core, y_lo * 4 + x)


def remote(src, dst, send, recv, target):
    return pltpu.make_async_remote_copy(
        src_ref=src, dst_ref=dst, send_sem=send, recv_sem=recv, device_id=target, device_id_type=MESH
    )


def fold_parity(value, top):
    while top:
        value = value ^ (value >> top)
        top //= 2
    return value & 1


def hadamard(length):
    rows = lax.broadcasted_iota(I32, (length, length), 0)
    cols = lax.broadcasted_iota(I32, (length, length), 1)
    return (1 - 2 * fold_parity(rows & cols, 8)).astype(F32).astype(BF16)


def split(value):
    high = value.astype(BF16)
    return high, (value - high.astype(F32)).astype(BF16)


def grad_kernel(
    x_ref, cot_ref, bits_ref, out_ref,
    gbuf, xbuf, xt, bits, own_sign, far_sign,
    a_send, a_recv, y_send, y_recv, x_send, x_recv, s_send, s_recv,
    b_send, b_recv, r_send, r_recv, c_send, c_recv, local_sem,
):
    _, narrow, y_hi, z, core, y_lo, x = place()
    real = narrow != LAST

    def dev(y_hi=y_hi, z=z, core=core, y_lo=y_lo, x=x):
        return device(y_hi, z, core, y_lo, x)

    z_up, z_down, z_far = (z + 1) % 4, (z + 3) % 4, (z + 2) % 4
    barrier = pltpu.get_barrier_semaphore()
    peers = [dev(y_lo=(narrow ^ o) // 4, x=(narrow ^ o) % 4) for o in range(1, 8)]
    peers += [dev(y_hi=1 - y_hi), dev(y_hi=1 - y_hi, y_lo=1 - y_lo)]
    peers += [dev(z=z_up), dev(z=z_down), dev(core=1 - core)]
    for peer in peers:
        pl.semaphore_signal(barrier, inc=1, device_id=peer, device_id_type=MESH)

    bits_copy = pltpu.make_async_copy(bits_ref.at[0], bits, local_sem.at[0])
    bits_copy.start()

    def slot(z_at, core_at, offset):
        return pl.ds(pl.multiple_of(((z_at * 2 + core_at) * 8 + (narrow ^ offset)) * TOK, TOK), TOK)

    def columns(index):
        return pl.ds(pl.multiple_of(index * COLS, COLS), COLS)

    own_copy = pltpu.make_async_copy(
        cot_ref.at[0, 0, :, columns(narrow)], gbuf.at[slot(z, core, 0)], local_sem.at[1]
    )

    @pl.when(real)
    def _():
        own_copy.start()

    pl.semaphore_wait(barrier, len(peers))

    def y_copy(target_lo):
        rel = y_hi ^ y_lo
        return remote(
            x_ref.at[0], xbuf.at[x, rel], y_send.at[target_lo], y_recv.at[rel],
            dev(y_hi=y_lo, y_lo=target_lo),
        )

    self_copy = pltpu.make_async_copy(x_ref.at[0], xbuf.at[x, 0], y_recv.at[0])
    for target_lo in range(2):
        mine = (y_hi == y_lo) & (y_lo == target_lo)

        @pl.when(mine)
        def _():
            self_copy.start()

        @pl.when(jnp.logical_not(mine))
        def _():
            y_copy(target_lo).start()

    def a_copy(offset):
        target = narrow ^ offset
        return remote(
            cot_ref.at[0, 0, :, columns(target)],
            gbuf.at[pl.ds(pl.multiple_of(((z * 2 + core) * 8 + narrow) * TOK, TOK), TOK)],
            a_send.at[offset], a_recv.at[offset],
            dev(y_lo=target // 4, x=target % 4),
        )

    for offset in range(1, 8):

        @pl.when((narrow ^ offset) != LAST)
        def _():
            a_copy(offset).start()

    bits_copy.wait()

    @pl.loop(0, ROWS // 16)
    def _(step):
        rows = pl.ds(pl.multiple_of(step * 16, 16), 16)
        own_sign[rows, :] = (2 * bits[rows, :] - 1).astype(F32).astype(BF16)

    def x_copy(rel, offset):
        return remote(
            xbuf.at[x, rel], xbuf.at[x, rel], x_send.at[rel, offset], x_recv.at[rel, offset],
            dev(x=x ^ offset),
        )

    for rel in range(2):
        if rel == 0:
            @pl.when(y_hi == y_lo)
            def _():
                self_copy.wait()

            @pl.when(y_hi != y_lo)
            def _():
                remote(x_ref.at[0], xbuf.at[x, 0], y_send.at[0], y_recv.at[0], dev(y_lo=1 - y_lo)).wait_recv()
        else:
            remote(x_ref.at[0], xbuf.at[x, 1], y_send.at[0], y_recv.at[1], dev(y_lo=1 - y_lo)).wait_recv()
        for offset in (1, 3, 2):
            x_copy(rel, offset).start()

    sign_copy = remote(own_sign, far_sign, s_send.at[0], s_recv.at[0], dev(y_hi=1 - y_hi))

    def ring_copy(direction, offset):
        rows = gbuf.at[slot(z, core, offset)]
        return remote(
            rows, rows, b_send.at[direction, offset], b_recv.at[direction, offset],
            dev(z=z_up if direction == 0 else z_down),
        )

    def relay_copy(direction, offset):
        source = z_down if direction == 0 else z_up
        base = ((source * 2 + core) * 8 + (narrow ^ offset)) * TOK + direction * (TOK // 2)
        rows = gbuf.at[pl.ds(pl.multiple_of(base, TOK // 2), TOK // 2)]
        return remote(
            rows, rows, r_send.at[direction, offset], r_recv.at[direction, offset],
            dev(z=z_up if direction == 0 else z_down),
        )

    z_of = (z, z_down, z_far, z_up)

    def core_copy(distance, offset):
        rows = gbuf.at[slot(z_of[distance], core, offset)]
        return remote(
            rows, rows, c_send.at[distance, offset], c_recv.at[distance, offset], dev(core=1 - core)
        )

    def multiply(distance, first, last):
        z_at = z_of[distance]

        @pl.when(x != z_at)
        def _():
            for rel in range(2):
                x_off = x ^ z_at
                remote(
                    xbuf.at[z_at, rel], xbuf.at[z_at, rel], x_send.at[rel, 1], x_recv.at[rel, x_off], dev(x=z_at)
                ).wait_recv()

        for offset in range(8):
            core_copy(distance, offset).wait_recv()
        for rel in range(2):
            xt[rel * ROWS:(rel + 1) * ROWS, :] = xbuf[z_at, rel].T
        tokens = pl.ds(pl.multiple_of(z_at * 512, 512), 512)

        @pl.loop(0, COLS // 256)
        def _(tile):
            cols = pl.ds(pl.multiple_of(tile * 256, 256), 256)
            part = jnp.dot(xt[...], gbuf[tokens, cols], preferred_element_type=F32)
            for rel, sign in ((0, own_sign), (1, far_sign)):
                value = part[rel * ROWS:(rel + 1) * ROWS]
                if not first:
                    value = value + out_ref[rel, :, cols]
                if last:
                    value = value * sign[:, cols].astype(F32)
                out_ref[rel, :, cols] = value

    @pl.when(real)
    def _():
        sign_copy.start()
        for offset in range(8):
            if offset == 0:
                own_copy.wait()
            else:
                remote(
                    cot_ref.at[0, 0, :, columns(narrow)], gbuf.at[slot(z, core, offset)],
                    a_send.at[offset], a_recv.at[offset], dev(core=1 - core),
                ).wait_recv()
            ring_copy(0, offset).start()
            ring_copy(1, offset).start()
            core_copy(0, offset).start()
        for offset in range(8):
            for direction in range(2):
                rows = gbuf.at[slot(z_down if direction == 0 else z_up, core, offset)]
                remote(
                    rows, rows, b_send.at[direction, offset], b_recv.at[direction, offset], dev(z=z_up)
                ).wait_recv()
                relay_copy(direction, offset).start()
                core_copy(1 if direction == 0 else 3, offset).start()
        multiply(0, True, False)
        multiply(1, False, False)
        multiply(3, False, False)
        for offset in range(8):
            for direction in range(2):
                base = ((z_far * 2 + core) * 8 + (narrow ^ offset)) * TOK + direction * (TOK // 2)
                rows = gbuf.at[pl.ds(pl.multiple_of(base, TOK // 2), TOK // 2)]
                remote(
                    rows, rows, r_send.at[direction, offset], r_recv.at[direction, offset], dev(z=z_up)
                ).wait_recv()
            core_copy(2, offset).start()
        sign_copy.wait_recv()
        multiply(2, False, True)
        sign_copy.wait_send()
        for offset in range(8):
            for direction in range(2):
                ring_copy(direction, offset).wait_send()
                relay_copy(direction, offset).wait_send()
            for distance in range(4):
                core_copy(distance, offset).wait_send()

    @pl.when(jnp.logical_not(real))
    def _():
        out_ref[...] = jnp.zeros_like(out_ref)
        for offset in range(1, 4):
            for rel in range(2):
                remote(
                    xbuf.at[x ^ offset, rel], xbuf.at[x ^ offset, rel], x_send.at[rel, 1], x_recv.at[rel, offset],
                    dev(x=x ^ offset),
                ).wait_recv()

    for rel in range(2):
        for offset in (1, 3, 2):
            x_copy(rel, offset).wait_send()
    for target_lo in range(2):
        mine = (y_hi == y_lo) & (y_lo == target_lo)

        @pl.when(jnp.logical_not(mine))
        def _():
            y_copy(target_lo).wait_send()

    for offset in range(1, 8):

        @pl.when((narrow ^ offset) != LAST)
        def _():
            a_copy(offset).wait_send()


def gradient(inputs, out_cotangent, sign_bits):
    any_spec = pl.BlockSpec(memory_space=pl.ANY)
    dma = pltpu.SemaphoreType.DMA
    return pl.pallas_call(
        grad_kernel,
        out_shape=jax.ShapeDtypeStruct((2, ROWS, COLS), F32),
        in_specs=[any_spec] * 3,
        out_specs=pl.BlockSpec(memory_space=pltpu.VMEM),
        scratch_shapes=[
            pltpu.VMEM((2048, COLS), BF16),
            pltpu.VMEM((4, 2, 512, ROWS), BF16),
            pltpu.VMEM((2 * ROWS, 512), BF16),
            pltpu.VMEM((ROWS, COLS), I32),
            pltpu.VMEM((ROWS, COLS), BF16),
            pltpu.VMEM((ROWS, COLS), BF16),
            dma((8,)), dma((8,)), dma((2,)), dma((2,)), dma((2, 4)), dma((2, 4)), dma((1,)), dma((1,)),
            dma((2, 8)), dma((2, 8)), dma((2, 8)), dma((2, 8)), dma((4, 8)), dma((4, 8)), dma((2,)),
        ],
        compiler_params=pltpu.CompilerParams(
            collective_id=0, has_side_effects=True, vmem_limit_bytes=VMEM_LIMIT
        ),
    )(inputs, out_cotangent, sign_bits)


def sample_kernel(index_ref, grad_ref, sign_ref, scale_ref, out_ref, table, rows):
    mix = hadamard(ROWS)
    for tile in range(8):
        done = []
        for rel in range(2):
            high, low = split(grad_ref[rel, :, 256 * tile:256 * (tile + 1)])
            done.append(jnp.dot(mix, high, preferred_element_type=F32) + jnp.dot(mix, low, preferred_element_type=F32))
        for rel, value in ((0, done[0] + done[1]), (1, done[0] - done[1])):
            left, right = value[:, :128], value[:, 128:]
            base = tile * 1024 + rel * ROWS
            table[base:base + ROWS, :] = left + right
            table[base + 512:base + 512 + ROWS, :] = left - right

    @pl.loop(0, 64)
    def _(step):
        start = pl.multiple_of(step * 8, 8)
        for half in range(2):
            value = [table[pl.ds((2 * tile + half) * 512 + start, 8), :] for tile in range(8)]
            for bit in (1, 2, 4):
                value = [
                    value[tile ^ bit] - value[tile] if tile & bit else value[tile] + value[tile | bit]
                    for tile in range(8)
                ]
            for tile in range(8):
                table[pl.ds((2 * tile + half) * 512 + start, 8), :] = value[tile]

    unroll = 32

    @pl.loop(0, 8192 // unroll)
    def _(step):
        base = pl.multiple_of(step * unroll, unroll)
        for i in range(unroll):
            rows[pl.ds(base + i, 1), :] = table[pl.ds(index_ref[base + i], 1), :]

    ones = jnp.ones((8, 128), BF16)
    last_dims = (((1,), (1,)), ((), ()))

    @pl.loop(0, 16)
    def _(step):
        span = pl.ds(pl.multiple_of(step * 512, 512), 512)
        high, low = split(rows[span, :] * sign_ref[span, :].astype(F32))
        total = lax.dot_general(ones, high, last_dims, preferred_element_type=F32)
        total = total + lax.dot_general(ones, low, last_dims, preferred_element_type=F32)
        for part in range(4):
            out_ref[step, part:part + 1, :] = total[0:1, part * 128:(part + 1) * 128] * scale_ref[step, part:part + 1, :]


def sample(index, grads, signs, scale):
    vmem = pl.BlockSpec(memory_space=pltpu.VMEM)
    return pl.pallas_call(
        sample_kernel,
        out_shape=jax.ShapeDtypeStruct((16, 4, 128), F32),
        in_specs=[pl.BlockSpec(memory_space=pltpu.SMEM), vmem, vmem, vmem],
        out_specs=vmem,
        scratch_shapes=[pltpu.VMEM((8192, 128), F32), pltpu.VMEM((8192, 128), F32)],
        compiler_params=pltpu.CompilerParams(vmem_limit_bytes=VMEM_LIMIT),
    )(index, grads, signs, scale)


def sum_kernel(term_ref, out_ref, first, partial, second, w_send, w_recv, n_send, n_recv):
    wide, narrow = lax.axis_index("wide"), lax.axis_index("narrow")
    barrier = pltpu.get_barrier_semaphore()
    for offset in range(1, 16):
        pl.semaphore_signal(barrier, inc=1, device_id=(wide ^ offset, narrow), device_id_type=MESH)
    for offset in range(1, 8):
        pl.semaphore_signal(barrier, inc=1, device_id=(wide, narrow ^ offset), device_id_type=MESH)
    pl.semaphore_wait(barrier, 22)

    def wide_copy(offset):
        return remote(
            term_ref.at[wide ^ offset], first.at[offset], w_send.at[offset], w_recv.at[offset], (wide ^ offset, narrow)
        )

    def narrow_copy(offset):
        target = narrow ^ offset
        return remote(
            partial.at[target // 2], second.at[offset], n_send.at[offset], n_recv.at[offset], (wide, target)
        )

    for offset in range(1, 16):
        wide_copy(offset).start()
    total = term_ref[wide]
    for offset in range(1, 16):
        wide_copy(offset).wait_recv()
        total = total + first[offset]
    for row in range(4):
        partial[row] = total[row:row + 1]
    for offset in range(1, 8):
        narrow_copy(offset).start()
    line = partial[narrow // 2]
    for offset in range(1, 8):
        narrow_copy(offset).wait_recv()
        line = line + second[offset]
    out_ref[0] = jnp.where(narrow % 2 == 1, line[:, 64:], line[:, :64])
    for offset in range(1, 16):
        wide_copy(offset).wait_send()
    for offset in range(1, 8):
        narrow_copy(offset).wait_send()


def sum_terms(terms):
    vmem = pl.BlockSpec(memory_space=pltpu.VMEM)
    dma = pltpu.SemaphoreType.DMA
    return pl.pallas_call(
        sum_kernel,
        out_shape=jax.ShapeDtypeStruct((1, 1, 64), F32),
        in_specs=[vmem],
        out_specs=vmem,
        scratch_shapes=[
            pltpu.VMEM((16, 4, 128), F32), pltpu.VMEM((4, 1, 128), F32), pltpu.VMEM((8, 1, 128), F32),
            dma((16,)), dma((16,)), dma((8,)), dma((8,)),
        ],
        compiler_params=pltpu.CompilerParams(
            collective_id=1, has_side_effects=True, vmem_limit_bytes=VMEM_LIMIT
        ),
    )(terms)


def body(inputs, out_cotangent, sign_bits, row_pick, col_pick):
    wide, narrow = lax.axis_index("wide"), lax.axis_index("narrow")
    row, col = row_pick[0], col_pick[0]
    index = (col // 128) % 16 * 512 + row // 2048 * 256 + row % 256
    parity = fold_parity((wide & (row // 256)) ^ (narrow & (col // 2048)), 8)
    scale = jnp.where(parity == 1, F32(-1.0), F32(1.0)) / jnp.sqrt(F32(row.shape[0]))
    lanes = jnp.arange(128, dtype=I32)
    signs = (1 - 2 * fold_parity((col % 128)[:, None] & lanes[None, :], 4)).astype(BF16)
    grads = gradient(inputs, out_cotangent, sign_bits)
    terms = sample(index, grads, signs, scale.reshape(16, 4, 128))
    return sum_terms(terms)


def solution(mesh):
    return jax.shard_map(
        body,
        mesh=mesh,
        in_specs=(
            P(None, "narrow", "wide"),
            P(None, None, ("wide", "narrow"), None),
            P(None, "wide", "narrow"),
            P(),
            P(),
        ),
        out_specs=P(None, None, ("wide", "narrow")),
        check_vma=False,
    )
```

time: 1120 us -> 106 us (0.09); the launches traced: 1110 us -> 105 us
  waiting for transfers between devices: 783 us -> 0 us
  local copies, waits for them, and re-layouts: 136 us -> 1.11 us
  Pallas kernels: 0 us -> 95.9 us
  other arithmetic: 92.2 us -> 8.02 us
  matrix products: 53.7 us -> 0 us
  blocking collectives: 20.9 us -> 0 us
  between operations: 13.7 us -> 0.02 us
    unnamed x4 -> x0, waiting for transfers between devices: 647 us -> none
    all_gather x2 -> x0, waiting for transfers between devices: 107 us -> none  [the longest x1 107 us: body(): lax.all_gather(column_cot, 'wide', axis=2, tiled=True)]
    pallas_call x0 -> x3, Pallas kernels: none -> 95.9 us  [the longest x1 65.6 us: gradient(): pl.pallas_call(grad_kernel, out_shape=jax.ShapeDtypeStruct((2, ROWS, COLS...]
    unnamed x1 -> x0, other arithmetic: 90.8 us -> none
    unnamed x16 -> x1, local copies, waits for them, and re-layouts: 58.4 us -> 1.11 us
    dot_general x5 -> x0, matrix products: 53.7 us -> none  [the longest x2 33.4 us: transform_last(): jnp.tensordot(shaped, hadamard(factor), axes=([leading + placed], [0]), p...]
    gather x1 -> x0, local copies, waits for them, and re-layouts: 45.5 us -> none  [body(): jnp.take_along_axis(finished.reshape(signed.shape[0], -1), lookup, axis=1)]
    all_to_all x1 -> x0, waiting for transfers between devices: 28.9 us -> none  [body(): lax.all_to_all(pieces, ('wide', 'narrow'), split_axis=1, concat_axis=1, t...]
  transfers between devices with their start and end apart: 4 -> 0, of which waited for: 3 -> 0; matrix products, arithmetic and copies ran while one was open for 14% -> 0% of each run, Pallas kernels for 0% -> 0%
where the time goes in v1:
time: 106 us; the launch traced here: 105 us
  Pallas kernels  95.9 us (90%)
  other arithmetic  8.02 us (8%)
  local copies, waits for them, and re-layouts  1.11 us (1%)
    pallas_call x1, Pallas kernels, gradient(): pl.pallas_call(grad_kernel, out_shape=jax.ShapeDtypeStruct((2, ROWS, COLS...  65.6 us
    pallas_call x1, Pallas kernels, sample(): pl.pallas_call(sample_kernel, out_shape=jax.ShapeDtypeStruct((16, 4, 128)...  16.7 us
    pallas_call x1, Pallas kernels, sum_terms(): pl.pallas_call(sum_kernel, out_shape=jax.ShapeDtypeStruct((1, 1, 64), F32...  13.5 us
    convert_element_type x1, other arithmetic, body(): (1 - 2 * fold_parity((col % 128)[:, None] & lanes[None, :], 4)).astype(BF16)  5.06 us

profile of v1, /device:TPU:0, one launch (start us, length us, event | category | flops | bytes accessed | tf_op | source)
XLA Modules:
  0.0 105.1 jit_solution(16260110207988086702)
XLA Ops:
  0.0 1.5 %select_multiply_fusion.scale_ref = f32[16,4,128]{2,1,0:T(4,128)} fusion(s32[16,4,128]{2,1,0:T(4,128)} %bitcast.4, s32[16,4,128]{2,1,0:T(4,128)} %bitcast.6, s32[]{:T(128)S(6)} %axis_index.25, s32[]{:T(128)S(6)} %axis_index.23), kind=kLoop, calls=%fused_computation.45 | loop fusion | flops 368640 | bytes 98312 | tf_op jit(solution)/shard_map/div | solution.py:428
  1.5 1.5 %add_select_fusion.2 = (s32[8192]{0:T(1024)S(1)}, s32[8192]{0:T(1024)}) fusion(s32[8192]{0:T(1024)} %bitcast.5, s32[8192]{0:T(1024)} %bitcast.7), kind=kLoop, calls=%fused_computation.19 | loop fusion | flops 466944 | bytes 131072 | tf_op jit(solution)/shard_map/jit(remainder)/select_n | solution.py:430
  3.0 5.1 %fusion.3.sign_ref = bf16[8192,128]{1,0:T(8,128)(2,1)} fusion(s32[8192]{0:T(1024)S(1)} %get-tuple-element.5), kind=kLoop, calls=%fused_computation.6 | loop fusion | flops 11534336 | bytes 2129920 | tf_op jit(solution)/shard_map/convert_element_type | solution.py:430
  8.0 65.6 %shard_map.55.grad_ref = f32[2,256,2048]{2,1,0:T(8,128)} custom-call(bf16[1,512,256]{2,1,0:T(8,128)(2,1)} %x_ref.1, bf16[1,1,32,14336]{3,2,1,0:T(8,128)(2,1)} %cot_ref.1, s32[1,256,2048]{2,1,0:T(8,128)} %bits_ref.1), custom_call_target="tpu_custom_call" | custom-call | tf_op jit(solution)/shard_map/pallas_call | solution.py:284
  73.7 16.7 %shard_map.56.term_ref = f32[16,4,128]{2,1,0:T(4,128)} custom-call(s32[8192]{0:T(1024)} %get-tuple-element.6.index_ref, f32[2,256,2048]{2,1,0:T(8,128)} %shard_map.55.grad_ref, bf16[8192,128]{1,0:T(8,128)(2,1)} %fusion.3.sign_ref, f32[16,4,128]{2,1,0:T(4,128)} %select_multiply_fusion.scale_ref), custom_call_target="tpu_custom_call" | custom-call | tf_op jit(solution)/shard_map/pallas_call | solution.py:354
  90.4 13.5 %shard_map.57 = f32[1,1,64]{2,1,0:T(1,128)} custom-call(f32[16,4,128]{2,1,0:T(4,128)} %shard_map.56.term_ref), custom_call_target="tpu_custom_call" | custom-call | tf_op jit(solution)/shard_map/pallas_call | solution.py:408
  104.0 1.1 %copy.7 = f32[1,1,64]{2,1,0:T(1,128)} copy(f32[1,1,64]{2,1,0:T(1,128)} %shard_map.57) | data formatting | bytes 512

commit v2 on v1

v2 whole, which is shorter than its diff:
```python
import functools

import jax
import jax.numpy as jnp
from jax import lax
from jax.experimental import pallas as pl
from jax.experimental.pallas import tpu as pltpu
from jax.sharding import PartitionSpec as P

MESH = pl.DeviceIdType.MESH
F32 = jnp.float32
BF16 = jnp.bfloat16
I32 = jnp.int32
VMEM_LIMIT = 60 << 20

TOK = 32
COLS = 2048
ROWS = 256
LAST = 7


def place():
    wide = lax.axis_index("wide")
    narrow = lax.axis_index("narrow")
    return wide, narrow, wide // 8, (wide // 2) % 4, wide % 2, narrow // 4, narrow % 4


def device(y_hi, z, core, y_lo, x):
    return (y_hi * 8 + z * 2 + core, y_lo * 4 + x)


def remote(src, dst, send, recv, target):
    return pltpu.make_async_remote_copy(
        src_ref=src, dst_ref=dst, send_sem=send, recv_sem=recv, device_id=target, device_id_type=MESH
    )


def fold_parity(value, top):
    while top:
        value = value ^ (value >> top)
        top //= 2
    return value & 1


def hadamard(length):
    rows = lax.broadcasted_iota(I32, (length, length), 0)
    cols = lax.broadcasted_iota(I32, (length, length), 1)
    return (1 - 2 * fold_parity(rows & cols, 8)).astype(F32).astype(BF16)


def split(value):
    high = value.astype(BF16)
    return high, (value - high.astype(F32)).astype(BF16)


def kernel(
    x_ref, cot_ref, bits_ref, row_ref, col_ref, out_ref,
    gbuf, xbuf, xt, bits, own_sign, far_sign, acc, table, rows, dot_sign, index_vmem, index, scale,
    terms, first, partial, second,
    a_send, a_recv, y_send, y_recv, x_send, x_recv, s_send, s_recv,
    b_send, b_recv, r_send, r_recv, c_send, c_recv, local_sem, w_send, w_recv, n_send, n_recv,
):
    wide, narrow, y_hi, z, core, y_lo, x = place()
    real = narrow != LAST

    def dev(y_hi=y_hi, z=z, core=core, y_lo=y_lo, x=x):
        return device(y_hi, z, core, y_lo, x)

    z_up, z_down, z_far = (z + 1) % 4, (z + 3) % 4, (z + 2) % 4
    barrier = pltpu.get_barrier_semaphore()
    peers = [(wide, narrow ^ offset) for offset in range(1, 8)]
    peers += [(wide ^ offset, narrow) for offset in range(1, 16)]
    peers += [dev(y_hi=1 - y_hi, y_lo=1 - y_lo)]
    for peer in peers:
        pl.semaphore_signal(barrier, inc=1, device_id=peer, device_id_type=MESH)

    def slot(z_at, core_at, offset):
        return pl.ds(pl.multiple_of(((z_at * 2 + core_at) * 8 + (narrow ^ offset)) * TOK, TOK), TOK)

    def columns(at):
        return pl.ds(pl.multiple_of(at * COLS, COLS), COLS)

    own_slice = cot_ref.at[0, 0, :, columns(narrow)]
    bits_copy = pltpu.make_async_copy(bits_ref.at[0], bits, local_sem.at[0])
    own_copy = pltpu.make_async_copy(own_slice, gbuf.at[slot(z, core, 0)], local_sem.at[1])
    index_copy = pltpu.make_async_copy(index_vmem, index, local_sem.at[2])
    bits_copy.start()

    @pl.when(real)
    def _():
        own_copy.start()

    row, col = row_ref[...], col_ref[...]
    index_vmem[...] = (col // 128) % 16 * 512 + row // 2048 * 256 + row % 256
    odd = fold_parity((wide & (row // 256)) ^ (narrow & (col // 2048)), 8)
    scale[...] = jnp.where(odd == 1, F32(-1.0), F32(1.0)) / jnp.sqrt(F32(8192))

    def ring_copy(direction, offset):
        landing = gbuf.at[slot(z, core, offset)]
        return remote(
            own_slice if offset == 0 else landing, landing,
            b_send.at[direction, offset], b_recv.at[direction, offset],
            dev(z=z_up if direction == 0 else z_down),
        )

    def relay_copy(direction, offset):
        source = z_down if direction == 0 else z_up
        base = ((source * 2 + core) * 8 + (narrow ^ offset)) * TOK + direction * (TOK // 2)
        span = gbuf.at[pl.ds(pl.multiple_of(base, TOK // 2), TOK // 2)]
        return remote(
            span, span, r_send.at[direction, offset], r_recv.at[direction, offset],
            dev(z=z_up if direction == 0 else z_down),
        )

    z_of = (z, z_down, z_far, z_up)

    def core_copy(distance, offset):
        landing = gbuf.at[slot(z_of[distance], core, offset)]
        return remote(
            own_slice if distance == 0 and offset == 0 else landing, landing,
            c_send.at[distance, offset], c_recv.at[distance, offset], dev(core=1 - core),
        )

    def pass_on(offset):
        ring_copy(0, offset).start()
        ring_copy(1, offset).start()
        core_copy(0, offset).start()

    pl.semaphore_wait(barrier, len(peers))

    @pl.when(real)
    def _():
        pass_on(0)

    def y_copy(target_lo):
        rel = y_hi ^ y_lo
        return remote(
            x_ref.at[0], xbuf.at[x, rel], y_send.at[target_lo], y_recv.at[rel],
            dev(y_hi=y_lo, y_lo=target_lo),
        )

    self_copy = pltpu.make_async_copy(x_ref.at[0], xbuf.at[x, 0], y_recv.at[0])
    for target_lo in range(2):
        mine = (y_hi == y_lo) & (y_lo == target_lo)

        @pl.when(mine)
        def _():
            self_copy.start()

        @pl.when(jnp.logical_not(mine))
        def _():
            y_copy(target_lo).start()

    def a_copy(offset):
        target = narrow ^ offset
        return remote(
            cot_ref.at[0, 0, :, columns(target)],
            gbuf.at[pl.ds(pl.multiple_of(((z * 2 + core) * 8 + narrow) * TOK, TOK), TOK)],
            a_send.at[offset], a_recv.at[offset],
            dev(y_lo=target // 4, x=target % 4),
        )

    order = (1, 3, 2, 4, 5, 7, 6)
    for offset in order:

        @pl.when((narrow ^ offset) != LAST)
        def _():
            a_copy(offset).start()

    index_copy.start()

    bits_copy.wait()

    @pl.loop(0, ROWS // 16)
    def _(step):
        span = pl.ds(pl.multiple_of(step * 16, 16), 16)
        own_sign[span, :] = (2 * bits[span, :] - 1).astype(F32).astype(BF16)

    sign_copy = remote(own_sign, far_sign, s_send.at[0], s_recv.at[0], dev(y_hi=1 - y_hi))

    def x_copy(rel, offset):
        return remote(
            xbuf.at[x, rel], xbuf.at[x, rel], x_send.at[rel, offset], x_recv.at[rel, offset],
            dev(x=x ^ offset),
        )

    def spread_inputs(rel):
        if rel == 0:
            @pl.when(y_hi == y_lo)
            def _():
                self_copy.wait()

            @pl.when(y_hi != y_lo)
            def _():
                remote(x_ref.at[0], xbuf.at[x, 0], y_send.at[0], y_recv.at[0], dev(y_lo=1 - y_lo)).wait_recv()
        else:
            remote(x_ref.at[0], xbuf.at[x, 1], y_send.at[0], y_recv.at[1], dev(y_lo=1 - y_lo)).wait_recv()
        for offset in (1, 3, 2):
            x_copy(rel, offset).start()

    lanes = lax.broadcasted_iota(I32, (128, 128), 1)

    def dot_signs(piece):
        for line in range(4 * piece, 4 * piece + 4):
            low = jnp.broadcast_to(col_ref[line:line + 1, :] % 128, (128, 128)).T
            dot_sign[line * 128:line * 128 + 128, :] = (1 - 2 * fold_parity(low & lanes, 4)).astype(F32).astype(BF16)

    def multiply(distance, start, last):
        z_at = z_of[distance]

        @pl.when(x != z_at)
        def _():
            for rel in range(2):
                landing = xbuf.at[z_at, rel]
                remote(landing, landing, x_send.at[rel, 1], x_recv.at[rel, x ^ z_at], dev(x=z_at)).wait_recv()

        for offset in range(8):
            core_copy(distance, offset).wait_recv()
        for rel in range(2):
            xt[rel * ROWS:(rel + 1) * ROWS, :] = xbuf[z_at, rel].T
        tokens = pl.ds(pl.multiple_of(z_at * 512, 512), 512)

        @pl.loop(0, COLS // 256)
        def _(tile):
            cols = pl.ds(pl.multiple_of(tile * 256, 256), 256)
            part = jnp.dot(xt[...], gbuf[tokens, cols], preferred_element_type=F32)
            for rel in range(2):
                value = part[rel * ROWS:(rel + 1) * ROWS]
                if not start:
                    value = value + acc[rel, :, cols]
                acc[rel, :, cols] = value

    def mix_rows(mix, rel, sign, cols):
        high, low = split(acc[rel, :, cols] * sign[:, cols].astype(F32))
        return jnp.dot(mix, high, preferred_element_type=F32) + jnp.dot(mix, low, preferred_element_type=F32)

    @pl.when(real)
    def _():
        sign_copy.start()
        for at, offset in enumerate(order):
            remote(
                own_slice, gbuf.at[slot(z, core, offset)], a_send.at[offset], a_recv.at[offset], dev(core=1 - core)
            ).wait_recv()
            pass_on(offset)
            if at in (2, 3):
                spread_inputs(at - 2)
            dot_signs(at)
        for at, offset in enumerate((0,) + order):
            for direction in range(2):
                landing = gbuf.at[slot(z_down if direction == 0 else z_up, core, offset)]
                remote(
                    landing, landing, b_send.at[direction, offset], b_recv.at[direction, offset], dev(z=z_up)
                ).wait_recv()
                relay_copy(direction, offset).start()
                core_copy(1 if direction == 0 else 3, offset).start()
            dot_signs(7 + at)
        own_copy.wait()
        multiply(0, True, False)
        multiply(1, False, False)
        multiply(3, False, False)
        dot_signs(15)
        for offset in (0,) + order:
            for direction in range(2):
                base = ((z_far * 2 + core) * 8 + (narrow ^ offset)) * TOK + direction * (TOK // 2)
                span = gbuf.at[pl.ds(pl.multiple_of(base, TOK // 2), TOK // 2)]
                remote(
                    span, span, r_send.at[direction, offset], r_recv.at[direction, offset], dev(z=z_up)
                ).wait_recv()
            core_copy(2, offset).start()
        multiply(2, False, True)

        mix = hadamard(ROWS)

        @pl.loop(0, 8)
        def _(tile):
            cols = pl.ds(pl.multiple_of(tile * 256, 256), 256)
            acc[0, :, cols] = mix_rows(mix, 0, own_sign, cols)

        sign_copy.wait_recv()

        @pl.loop(0, 8)
        def _(tile):
            cols = pl.ds(pl.multiple_of(tile * 256, 256), 256)
            near, far = acc[0, :, cols], mix_rows(mix, 1, far_sign, cols)
            for rel, value in ((0, near + far), (1, near - far)):
                left, right = value[:, :128], value[:, 128:]
                base = pl.multiple_of(tile * 1024 + rel * ROWS, ROWS)
                table[pl.ds(base, ROWS), :] = left + right
                table[pl.ds(base + 512, ROWS), :] = left - right

        @pl.loop(0, 64)
        def _(step):
            start = pl.multiple_of(step * 8, 8)
            for half in range(2):
                value = [table[pl.ds((2 * tile + half) * 512 + start, 8), :] for tile in range(8)]
                for bit in (1, 2, 4):
                    value = [
                        value[tile ^ bit] - value[tile] if tile & bit else value[tile] + value[tile | bit]
                        for tile in range(8)
                    ]
                for tile in range(8):
                    table[pl.ds((2 * tile + half) * 512 + start, 8), :] = value[tile]

        index_copy.wait()

        @pl.loop(0, 64)
        def _(line):
            base = pl.multiple_of(line * 128, 128)
            for i in range(128):
                rows[pl.ds(base + i, 1), :] = table[pl.ds(index[line, i], 1), :]

        ones = jnp.ones((8, 128), BF16)
        last_dims = (((1,), (1,)), ((), ()))

        @pl.loop(0, 16)
        def _(step):
            span = pl.ds(pl.multiple_of(step * 512, 512), 512)
            high, low = split(rows[span, :] * dot_sign[span, :].astype(F32))
            total = lax.dot_general(ones, high, last_dims, preferred_element_type=F32)
            total = total + lax.dot_general(ones, low, last_dims, preferred_element_type=F32)
            for part in range(4):
                terms[step, part:part + 1, :] = (
                    total[0:1, part * 128:(part + 1) * 128] * scale[pl.ds(step * 4 + part, 1), :]
                )

    @pl.when(jnp.logical_not(real))
    def _():
        index_copy.wait()
        terms[...] = jnp.zeros_like(terms)
        for rel in range(2):
            spread_inputs(rel)
        for offset in range(1, 4):
            for rel in range(2):
                landing = xbuf.at[x ^ offset, rel]
                remote(landing, landing, x_send.at[rel, 1], x_recv.at[rel, offset], dev(x=x ^ offset)).wait_recv()

    def wide_copy(offset):
        return remote(
            terms.at[wide ^ offset], first.at[offset], w_send.at[offset], w_recv.at[offset], (wide ^ offset, narrow)
        )

    def narrow_copy(offset):
        target = narrow ^ offset
        return remote(
            partial.at[target // 2], second.at[offset], n_send.at[offset], n_recv.at[offset], (wide, target)
        )

    for offset in range(1, 16):
        wide_copy(offset).start()
    total = terms[wide]
    for offset in range(1, 16):
        wide_copy(offset).wait_recv()
        total = total + first[offset]
    for line in range(4):
        partial[line] = total[line:line + 1]
    for offset in range(1, 8):
        narrow_copy(offset).start()
    line = partial[narrow // 2]
    for offset in range(1, 8):
        narrow_copy(offset).wait_recv()
        line = line + second[offset]
    out_ref[0] = jnp.where(narrow % 2 == 1, line[:, 64:], line[:, :64])

    @pl.when(real)
    def _():
        sign_copy.wait_send()
        for offset in range(8):
            for direction in range(2):
                ring_copy(direction, offset).wait_send()
                relay_copy(direction, offset).wait_send()
            for distance in range(4):
                core_copy(distance, offset).wait_send()

    for rel in range(2):
        for offset in (1, 3, 2):
            x_copy(rel, offset).wait_send()
    for target_lo in range(2):
        mine = (y_hi == y_lo) & (y_lo == target_lo)

        @pl.when(jnp.logical_not(mine))
        def _():
            y_copy(target_lo).wait_send()

    for offset in range(1, 8):

        @pl.when((narrow ^ offset) != LAST)
        def _():
            a_copy(offset).wait_send()

    for offset in range(1, 16):
        wide_copy(offset).wait_send()
    for offset in range(1, 8):
        narrow_copy(offset).wait_send()


def body(inputs, out_cotangent, sign_bits, row_pick, col_pick):
    hbm = pl.BlockSpec(memory_space=pl.ANY)
    vmem = pl.BlockSpec(memory_space=pltpu.VMEM)
    dma = pltpu.SemaphoreType.DMA
    return pl.pallas_call(
        kernel,
        out_shape=jax.ShapeDtypeStruct((1, 1, 64), F32),
        in_specs=[hbm, hbm, hbm, vmem, vmem],
        out_specs=vmem,
        scratch_shapes=[
            pltpu.VMEM((2048, COLS), BF16),
            pltpu.VMEM((4, 2, 512, ROWS), BF16),
            pltpu.VMEM((2 * ROWS, 512), BF16),
            pltpu.VMEM((ROWS, COLS), I32),
            pltpu.VMEM((ROWS, COLS), BF16),
            pltpu.VMEM((ROWS, COLS), BF16),
            pltpu.VMEM((2, ROWS, COLS), F32),
            pltpu.VMEM((8192, 128), F32),
            pltpu.VMEM((8192, 128), F32),
            pltpu.VMEM((8192, 128), BF16),
            pltpu.VMEM((64, 128), I32),
            pltpu.SMEM((64, 128), I32),
            pltpu.VMEM((64, 128), F32),
            pltpu.VMEM((16, 4, 128), F32),
            pltpu.VMEM((16, 4, 128), F32),
            pltpu.VMEM((4, 1, 128), F32),
            pltpu.VMEM((8, 1, 128), F32),
            dma((8,)), dma((8,)), dma((2,)), dma((2,)), dma((2, 4)), dma((2, 4)), dma((1,)), dma((1,)),
            dma((2, 8)), dma((2, 8)), dma((2, 8)), dma((2, 8)), dma((4, 8)), dma((4, 8)), dma((3,)),
            dma((16,)), dma((16,)), dma((8,)), dma((8,)),
        ],
        compiler_params=pltpu.CompilerParams(
            collective_id=0, has_side_effects=True, vmem_limit_bytes=VMEM_LIMIT
        ),
    )(inputs, out_cotangent, sign_bits, row_pick.reshape(64, 128), col_pick.reshape(64, 128))


def solution(mesh):
    return jax.shard_map(
        body,
        mesh=mesh,
        in_specs=(
            P(None, "narrow", "wide"),
            P(None, None, ("wide", "narrow"), None),
            P(None, "wide", "narrow"),
            P(),
            P(),
        ),
        out_specs=P(None, None, ("wide", "narrow")),
        check_vma=False,
    )
```

time: 106 us -> 86.8 us (0.82)
  Pallas kernels: 95.9 us -> 85.4 us
  other arithmetic: 8.02 us -> 0 us
    pallas_call x3 -> x1, Pallas kernels: 95.9 us -> 85.4 us  [body(): pl.pallas_call(kernel, out_shape=jax.ShapeDtypeStruct((1, 1, 64), F32), i...]
    convert_element_type x1 -> x0, other arithmetic: 5.06 us -> none  [body(): (1 - 2 * fold_parity((col % 128)[:, None] & lanes[None, :], 4)).astype(BF16)]
    div x1 -> x0, other arithmetic: 1.5 us -> none  [body(): jnp.where(parity == 1, F32(-1.0), F32(1.0)) / jnp.sqrt(F32(row.shape[0]))]
    select_n x1 -> x0, other arithmetic: 1.46 us -> none  [body(): col % 128]
where the time goes in v2:
time: 86.8 us; the launch traced here: 86.6 us
  Pallas kernels  85.4 us (98%)
  local copies, waits for them, and re-layouts  1.19 us (1%)
    pallas_call x1, Pallas kernels, body(): pl.pallas_call(kernel, out_shape=jax.ShapeDtypeStruct((1, 1, 64), F32), i...  85.4 us

profile of v2, /device:TPU:0, one launch (start us, length us, event | category | flops | bytes accessed | tf_op | source)
XLA Modules:
  0.0 86.6 jit_solution(4085663715231861095)
XLA Ops:
  0.0 85.4 %shard_map.55 = f32[1,1,64]{2,1,0:T(1,128)} custom-call(bf16[1,512,256]{2,1,0:T(8,128)(2,1)} %x_ref.1, bf16[1,1,32,14336]{3,2,1,0:T(8,128)(2,1)} %cot_ref.1, s32[1,256,2048]{2,1,0:T(8,128)} %bits_ref.1, s32[64,128]{1,0:T(8,128)} %bitcast.2, s32[64,128]{1,0:T(8,128)} %bitcast.3), custom_call_target="tpu_custom_call" | custom-call | tf_op jit(solution)/shard_map/pallas_call | solution.py:400
  85.4 1.2 %copy.7 = f32[1,1,64]{2,1,0:T(1,128)} copy(f32[1,1,64]{2,1,0:T(1,128)} %shard_map.55) | data formatting | bytes 512

commit v3 on v2

v3 whole, which is shorter than its diff:
```python
import functools

import jax
import jax.numpy as jnp
from jax import lax
from jax.experimental import pallas as pl
from jax.experimental.pallas import tpu as pltpu
from jax.sharding import PartitionSpec as P

MESH = pl.DeviceIdType.MESH
F32 = jnp.float32
BF16 = jnp.bfloat16
I32 = jnp.int32
VMEM_LIMIT = 60 << 20

TOK = 32
COLS = 2048
ROWS = 256
SLICES = ((0, 1), (3, 2), (4, 5), (7,), (6,))
MULTIPLY_AT = (7, 9, 11, 12, 12)
LAST = 7


def place():
    wide = lax.axis_index("wide")
    narrow = lax.axis_index("narrow")
    return wide, narrow, wide // 8, (wide // 2) % 4, wide % 2, narrow // 4, narrow % 4


def device(y_hi, z, core, y_lo, x):
    return (y_hi * 8 + z * 2 + core, y_lo * 4 + x)


def remote(src, dst, send, recv, target):
    return pltpu.make_async_remote_copy(
        src_ref=src, dst_ref=dst, send_sem=send, recv_sem=recv, device_id=target, device_id_type=MESH
    )


def fold_parity(value, top):
    while top:
        value = value ^ (value >> top)
        top //= 2
    return value & 1


def hadamard(length):
    rows = lax.broadcasted_iota(I32, (length, length), 0)
    cols = lax.broadcasted_iota(I32, (length, length), 1)
    return (1 - 2 * fold_parity(rows & cols, 8)).astype(F32).astype(BF16)


def split(value):
    high = value.astype(BF16)
    return high, (value - high.astype(F32)).astype(BF16)


def kernel(
    inputs, cot_ref, bits_ref, row_ref, col_ref, out_ref,
    gbuf, xbuf, xt, bits, own_sign, far_sign, acc, table, rows, dot_sign, index_vmem, index, scale,
    terms, first, partial, second,
    a_send, a_recv, y_send, y_recv, x_send, x_recv, h_send, h_recv, s_send, s_recv,
    b_send, b_recv, r_send, r_recv, c_send, c_recv, local_sem, w_send, w_recv, n_send, n_recv,
):
    wide, narrow, y_hi, z, core, y_lo, x = place()
    real = narrow != LAST

    def dev(y_hi=y_hi, z=z, core=core, y_lo=y_lo, x=x):
        return device(y_hi, z, core, y_lo, x)

    z_up, z_down, z_far = (z + 1) % 4, (z + 3) % 4, (z + 2) % 4
    barrier = pltpu.get_barrier_semaphore()
    peers = [(wide, narrow ^ offset) for offset in range(1, 8)]
    peers += [(wide ^ offset, narrow) for offset in range(1, 16)]
    peers += [dev(y_hi=1 - y_hi, y_lo=1 - y_lo)]
    for peer in peers:
        pl.semaphore_signal(barrier, inc=1, device_id=peer, device_id_type=MESH)

    def slot(z_at, core_at, offset):
        return gbuf.at[z_at * 2 + core_at, pl.ds(pl.multiple_of((narrow ^ offset) * TOK, TOK), TOK)]

    def half_slot(direction, z_at, offset):
        base = (narrow ^ offset) * TOK + direction * (TOK // 2)
        return gbuf.at[z_at * 2 + core, pl.ds(pl.multiple_of(base, TOK // 2), TOK // 2)]

    def columns(at):
        return pl.ds(pl.multiple_of(at * COLS, COLS), COLS)

    own_slice = cot_ref.at[0, 0, :, columns(narrow)]
    bits_copy = pltpu.make_async_copy(bits_ref.at[0], bits, local_sem.at[0])
    own_copy = pltpu.make_async_copy(own_slice, slot(z, core, 0), local_sem.at[1])
    index_copy = pltpu.make_async_copy(index_vmem, index, local_sem.at[2])
    bits_copy.start()

    @pl.when(real)
    def _():
        own_copy.start()

    row, col = row_ref[...], col_ref[...]
    index_vmem[...] = (col // 128) % 16 * 512 + row // 2048 * 256 + row % 256
    odd = fold_parity((wide & (row // 256)) ^ (narrow & (col // 2048)), 8)
    scale[...] = jnp.where(odd == 1, F32(-1.0), F32(1.0)) / jnp.sqrt(F32(8192))

    def ring_copy(direction, offset):
        landing = slot(z, core, offset)
        return remote(
            own_slice if offset == 0 else landing, landing,
            b_send.at[direction, offset], b_recv.at[direction, offset],
            dev(z=z_up if direction == 0 else z_down),
        )

    def relay_copy(direction, offset):
        span = half_slot(direction, z_down if direction == 0 else z_up, offset)
        return remote(
            span, span, r_send.at[direction, offset], r_recv.at[direction, offset],
            dev(z=z_up if direction == 0 else z_down),
        )

    z_of = (z, z_down, z_far, z_up)

    def core_copy(distance, offset):
        landing = slot(z_of[distance], core, offset)
        return remote(
            own_slice if distance == 0 and offset == 0 else landing, landing,
            c_send.at[distance, offset], c_recv.at[distance, offset], dev(core=1 - core),
        )

    def pass_on(offset):
        ring_copy(0, offset).start()
        ring_copy(1, offset).start()
        core_copy(0, offset).start()

    pl.semaphore_wait(barrier, len(peers))

    @pl.when(real)
    def _():
        pass_on(0)

    def y_copy(target_lo):
        rel = y_hi ^ y_lo
        return remote(
            inputs, xbuf.at[x, rel], y_send.at[target_lo], y_recv.at[rel],
            dev(y_hi=y_lo, y_lo=target_lo),
        )

    self_copy = pltpu.make_async_copy(inputs, xbuf.at[x, 0], y_recv.at[0])
    for target_lo in range(2):
        mine = (y_hi == y_lo) & (y_lo == target_lo)

        @pl.when(mine)
        def _():
            self_copy.start()

        @pl.when(jnp.logical_not(mine))
        def _():
            y_copy(target_lo).start()

    def a_copy(offset):
        target = narrow ^ offset
        return remote(
            cot_ref.at[0, 0, :, columns(target)],
            slot(z, core, 0),
            a_send.at[offset], a_recv.at[offset],
            dev(y_lo=target // 4, x=target % 4),
        )

    order = (0, 1, 3, 2, 4, 5, 7, 6)

    def send_cotangents(offsets):
        for offset in offsets:

            @pl.when((narrow ^ offset) != LAST)
            def _():
                a_copy(offset).start()

    send_cotangents(order[1:5])

    index_copy.start()

    bits_copy.wait()

    @pl.loop(0, ROWS // 16)
    def _(step):
        span = pl.ds(pl.multiple_of(step * 16, 16), 16)
        own_sign[span, :] = (2 * bits[span, :] - 1).astype(F32).astype(BF16)

    sign_copy = remote(own_sign, far_sign, s_send.at[0], s_recv.at[0], dev(y_hi=1 - y_hi))

    def x_copy(rel, offset):
        block = xbuf.at[x, rel]
        return remote(block, block, x_send.at[rel, offset], x_recv.at[rel, offset], dev(x=x ^ offset))

    def x_relay(rel, half):
        block = xbuf.at[x ^ (1 + 2 * half), rel, half]
        return remote(block, block, h_send.at[rel, half], h_recv.at[rel, half], dev(x=x ^ (3 - 2 * half)))

    def spread_inputs(rel):
        if rel == 0:
            @pl.when(y_hi == y_lo)
            def _():
                self_copy.wait()

            @pl.when(y_hi != y_lo)
            def _():
                remote(inputs, xbuf.at[x, 0], y_send.at[0], y_recv.at[0], dev(y_lo=1 - y_lo)).wait_recv()
        else:
            remote(inputs, xbuf.at[x, 1], y_send.at[0], y_recv.at[1], dev(y_lo=1 - y_lo)).wait_recv()
        for offset in (1, 3):
            x_copy(rel, offset).start()

    def relay_inputs(rel):
        for half in range(2):
            block = xbuf.at[x ^ (1 + 2 * half), rel]
            remote(
                block, block, x_send.at[rel, 1], x_recv.at[rel, 1 + 2 * half], dev(x=x ^ 1)
            ).wait_recv()
            x_relay(rel, half).start()

    def await_inputs():
        for rel in range(2):
            for half in range(2):
                block = xbuf.at[x ^ 2, rel, half]
                remote(block, block, h_send.at[rel, half], h_recv.at[rel, half], dev(x=x ^ 1)).wait_recv()

    lanes = lax.broadcasted_iota(I32, (128, 128), 1)

    def dot_signs(piece):
        for line in range(4 * piece, 4 * piece + 4):
            low = jnp.broadcast_to(col_ref[line:line + 1, :] % 128, (128, 128)).T
            dot_sign[line * 128:line * 128 + 128, :] = (1 - 2 * fold_parity(low & lanes, 4)).astype(F32).astype(BF16)

    def multiply(offsets):
        for distance in range(4):
            for offset in offsets:
                core_copy(distance, offset).wait_recv()
        size = len(offsets) * TOK
        tokens = pl.ds(pl.multiple_of((narrow ^ offsets[0]) // len(offsets) * size, size), size)
        depth = 8 * size
        for rel in range(2):
            xt[rel * ROWS:(rel + 1) * ROWS, :depth] = xbuf[:, rel, :, tokens, :].reshape(depth, ROWS).T

        @pl.loop(0, COLS // 256)
        def _(tile):
            cols = pl.ds(pl.multiple_of(tile * 256, 256), 256)
            part = jnp.dot(xt[:, :depth], gbuf[:, tokens, cols].reshape(depth, 256), preferred_element_type=F32)
            for rel in range(2):
                value = part[rel * ROWS:(rel + 1) * ROWS]
                if 0 not in offsets:
                    value = value + acc[rel, :, cols]
                acc[rel, :, cols] = value

    def wide_copy(offset):
        return remote(
            terms.at[wide ^ offset], first.at[offset], w_send.at[offset], w_recv.at[offset], (wide ^ offset, narrow)
        )

    def mix_rows(mix, rel, sign, cols):
        high, low = split(acc[rel, :, cols] * sign[:, cols].astype(F32))
        return jnp.dot(mix, high, preferred_element_type=F32) + jnp.dot(mix, low, preferred_element_type=F32)

    @pl.when(real)
    def _():
        sign_copy.start()
        for step in range(1, 13):
            if step < 8:
                remote(
                    own_slice, slot(z, core, order[step]), a_send.at[order[step]], a_recv.at[order[step]],
                    dev(core=1 - core),
                ).wait_recv()
                pass_on(order[step])
            if step in (2, 3):
                spread_inputs(step - 2)
                send_cotangents(order[5:6] if step == 2 else order[6:])
            if step in (4, 5):
                relay_inputs(step - 4)
            if 0 <= step - 2 < 8:
                offset = order[step - 2]
                for direction in range(2):
                    landing = slot(z_down if direction == 0 else z_up, core, offset)
                    remote(
                        landing, landing, b_send.at[direction, offset], b_recv.at[direction, offset], dev(z=z_up)
                    ).wait_recv()
                    relay_copy(direction, offset).start()
                    core_copy(1 if direction == 0 else 3, offset).start()
            if 0 <= step - 5 < 8:
                offset = order[step - 5]
                for direction in range(2):
                    span = half_slot(direction, z_far, offset)
                    remote(
                        span, span, r_send.at[direction, offset], r_recv.at[direction, offset], dev(z=z_up)
                    ).wait_recv()
                core_copy(2, offset).start()
            if step <= 8:
                dot_signs(2 * step - 2)
                dot_signs(2 * step - 1)
            if step == MULTIPLY_AT[0]:
                own_copy.wait()
                await_inputs()
            for at, offsets in zip(MULTIPLY_AT, SLICES, strict=True):
                if step == at:
                    multiply(offsets)

        mix = hadamard(ROWS)

        @pl.loop(0, 8)
        def _(tile):
            cols = pl.ds(pl.multiple_of(tile * 256, 256), 256)
            acc[0, :, cols] = mix_rows(mix, 0, own_sign, cols)

        sign_copy.wait_recv()

        @pl.loop(0, 8)
        def _(tile):
            cols = pl.ds(pl.multiple_of(tile * 256, 256), 256)
            near, far = acc[0, :, cols], mix_rows(mix, 1, far_sign, cols)
            for rel, value in ((0, near + far), (1, near - far)):
                left, right = value[:, :128], value[:, 128:]
                base = pl.multiple_of(tile * 1024 + rel * ROWS, ROWS)
                table[pl.ds(base, ROWS), :] = left + right
                table[pl.ds(base + 512, ROWS), :] = left - right

        @pl.loop(0, 64)
        def _(step):
            start = pl.multiple_of(step * 8, 8)
            for half in range(2):
                value = [table[pl.ds((2 * tile + half) * 512 + start, 8), :] for tile in range(8)]
                for bit in (1, 2, 4):
                    value = [
                        value[tile ^ bit] - value[tile] if tile & bit else value[tile] + value[tile | bit]
                        for tile in range(8)
                    ]
                for tile in range(8):
                    table[pl.ds((2 * tile + half) * 512 + start, 8), :] = value[tile]

        index_copy.wait()
        ones = jnp.ones((8, 256), BF16)
        last_dims = (((1,), (1,)), ((), ()))

        def dot_rows(block, held):
            span = pl.ds(pl.multiple_of(block * 512, 512), 512)
            both = jnp.concatenate(split(held[...] * dot_sign[span, :].astype(F32)), axis=1)
            total = lax.dot_general(ones, both, last_dims, preferred_element_type=F32)
            for part in range(4):
                terms[block, part:part + 1, :] = (
                    total[0:1, part * 128:(part + 1) * 128] * scale[pl.ds(block * 4 + part, 1), :]
                )

        @pl.loop(0, 16)
        def _(step):
            block = wide ^ (15 - step)

            @pl.loop(0, 4)
            def _(part):
                base = pl.multiple_of(part * 128, 128)
                for i in range(128):
                    rows[0, pl.ds(base + i, 1), :] = table[pl.ds(index[block * 4 + part, i], 1), :]

            dot_rows(block, rows.at[0])

            @pl.when(step < 15)
            def _():
                wide_copy(15 - step).start()

    @pl.when(jnp.logical_not(real))
    def _():
        index_copy.wait()
        terms[...] = jnp.zeros_like(terms)

        @pl.loop(1, 16)
        def _(step):
            wide_copy(16 - step).start()

        for rel in range(2):
            spread_inputs(rel)
            send_cotangents(order[5:6] if rel == 0 else order[6:])
        for rel in range(2):
            relay_inputs(rel)
        await_inputs()

    def narrow_copy(offset):
        target = narrow ^ offset
        return remote(
            partial.at[target // 2], second.at[offset], n_send.at[offset], n_recv.at[offset], (wide, target)
        )

    total = terms[wide]
    for offset in range(15, 0, -1):
        wide_copy(offset).wait_recv()
        total = total + first[offset]
    for line in range(4):
        partial[line] = total[line:line + 1]
    for offset in range(1, 8):
        narrow_copy(offset).start()
    line = partial[narrow // 2]
    for offset in range(1, 8):
        narrow_copy(offset).wait_recv()
        line = line + second[offset]
    out_ref[0] = jnp.where(narrow % 2 == 1, line[:, 64:], line[:, :64])

    @pl.when(real)
    def _():
        sign_copy.wait_send()
        for offset in order:
            for direction in range(2):
                ring_copy(direction, offset).wait_send()
                relay_copy(direction, offset).wait_send()
            for distance in range(4):
                core_copy(distance, offset).wait_send()

    for rel in range(2):
        for half in range(2):
            x_copy(rel, 1 + 2 * half).wait_send()
            x_relay(rel, half).wait_send()
    for target_lo in range(2):
        mine = (y_hi == y_lo) & (y_lo == target_lo)

        @pl.when(jnp.logical_not(mine))
        def _():
            y_copy(target_lo).wait_send()

    for offset in range(1, 8):

        @pl.when((narrow ^ offset) != LAST)
        def _():
            a_copy(offset).wait_send()

    for offset in range(1, 16):
        wide_copy(offset).wait_send()
    for offset in range(1, 8):
        narrow_copy(offset).wait_send()


def body(inputs, out_cotangent, sign_bits, row_pick, col_pick):
    hbm = pl.BlockSpec(memory_space=pl.ANY)
    vmem = pl.BlockSpec(memory_space=pltpu.VMEM)
    dma = pltpu.SemaphoreType.DMA
    return pl.pallas_call(
        kernel,
        out_shape=jax.ShapeDtypeStruct((1, 1, 64), F32),
        in_specs=[hbm, hbm, hbm, vmem, vmem],
        out_specs=vmem,
        scratch_shapes=[
            pltpu.VMEM((8, 8 * TOK, COLS), BF16),
            pltpu.VMEM((4, 2, 2, 8 * TOK, ROWS), BF16),
            pltpu.VMEM((2 * ROWS, 512), BF16),
            pltpu.VMEM((ROWS, COLS), I32),
            pltpu.VMEM((ROWS, COLS), BF16),
            pltpu.VMEM((ROWS, COLS), BF16),
            pltpu.VMEM((2, ROWS, COLS), F32),
            pltpu.VMEM((8192, 128), F32),
            pltpu.VMEM((2, 512, 128), F32),
            pltpu.VMEM((8192, 128), BF16),
            pltpu.VMEM((64, 128), I32),
            pltpu.SMEM((64, 128), I32),
            pltpu.VMEM((64, 128), F32),
            pltpu.VMEM((16, 4, 128), F32),
            pltpu.VMEM((16, 4, 128), F32),
            pltpu.VMEM((4, 1, 128), F32),
            pltpu.VMEM((8, 1, 128), F32),
            dma((8,)), dma((8,)), dma((2,)), dma((2,)), dma((2, 4)), dma((2, 4)), dma((2, 2)), dma((2, 2)), dma((1,)), dma((1,)),
            dma((2, 8)), dma((2, 8)), dma((2, 8)), dma((2, 8)), dma((4, 8)), dma((4, 8)), dma((3,)),
            dma((16,)), dma((16,)), dma((8,)), dma((8,)),
        ],
        compiler_params=pltpu.CompilerParams(
            collective_id=0, has_side_effects=True, vmem_limit_bytes=VMEM_LIMIT
        ),
    )(inputs.reshape(2, 8 * TOK, ROWS), out_cotangent, sign_bits, row_pick.reshape(64, 128), col_pick.reshape(64, 128))


def solution(mesh):
    return jax.shard_map(
        body,
        mesh=mesh,
        in_specs=(
            P(None, "narrow", "wide"),
            P(None, None, ("wide", "narrow"), None),
            P(None, "wide", "narrow"),
            P(),
            P(),
        ),
        out_specs=P(None, None, ("wide", "narrow")),
        check_vma=False,
    )
```

time: 86.8 us -> 79.3 us (0.914)
  Pallas kernels: 85.4 us -> 77.9 us
    pallas_call x1, Pallas kernels: 85.4 us -> 77.9 us  [body(): pl.pallas_call(kernel, out_shape=jax.ShapeDtypeStruct((1, 1, 64), F32), i...]
where the time goes in v3:
time: 79.3 us; the launch traced here: 79.1 us
  Pallas kernels  77.9 us (98%)
  local copies, waits for them, and re-layouts  1.19 us (2%)
    pallas_call x1, Pallas kernels, body(): pl.pallas_call(kernel, out_shape=jax.ShapeDtypeStruct((1, 1, 64), F32), i...  77.9 us

profile of v3, /device:TPU:0, one launch (start us, length us, event | category | flops | bytes accessed | tf_op | source)
XLA Modules:
  0.0 79.1 jit_solution(11888509043014133949)
XLA Ops:
  0.0 77.9 %shard_map.55 = f32[1,1,64]{2,1,0:T(1,128)} custom-call(bf16[2,256,256]{2,1,0:T(8,128)(2,1)} %bitcast.3, bf16[1,1,32,14336]{3,2,1,0:T(8,128)(2,1)} %cot_ref.1, s32[1,256,2048]{2,1,0:T(8,128)} %bits_ref.1, s32[64,128]{1,0:T(8,128)} %bitcast.4, s32[64,128]{1,0:T(8,128)} %bitcast.5), custom_call_target="tpu_custom_call" | custom-call | tf_op jit(solution)/shard_map/pallas_call | solution.py:437
  77.9 1.2 %copy.7 = f32[1,1,64]{2,1,0:T(1,128)} copy(f32[1,1,64]{2,1,0:T(1,128)} %shard_map.55) | data formatting | bytes 512

commit v4 on v3

--- a/solution.py
+++ b/solution.py
@@ -255,8 +255,8 @@
         )
 
     def mix_rows(mix, rel, sign, cols):
-        high, low = split(acc[rel, :, cols] * sign[:, cols].astype(F32))
-        return jnp.dot(mix, high, preferred_element_type=F32) + jnp.dot(mix, low, preferred_element_type=F32)
+        both = jnp.concatenate(split(acc[rel, :, cols] * sign[:, cols].astype(F32)), axis=0)
+        return jnp.dot(mix, both, preferred_element_type=F32)
 
     @pl.when(real)
     def _():
@@ -300,7 +300,7 @@
                 if step == at:
                     multiply(offsets)
 
-        mix = hadamard(ROWS)
+        mix = jnp.concatenate([hadamard(ROWS)] * 2, axis=1)
 
         @pl.loop(0, 8)
         def _(tile):
@@ -333,16 +333,13 @@
                     table[pl.ds((2 * tile + half) * 512 + start, 8), :] = value[tile]
 
         index_copy.wait()
-        ones = jnp.ones((8, 256), BF16)
-        last_dims = (((1,), (1,)), ((), ()))
 
         def dot_rows(block, held):
             span = pl.ds(pl.multiple_of(block * 512, 512), 512)
-            both = jnp.concatenate(split(held[...] * dot_sign[span, :].astype(F32)), axis=1)
-            total = lax.dot_general(ones, both, last_dims, preferred_element_type=F32)
+            total = jnp.sum((held[...] * dot_sign[span, :].astype(F32)).T, axis=0, keepdims=True)
             for part in range(4):
                 terms[block, part:part + 1, :] = (
-                    total[0:1, part * 128:(part + 1) * 128] * scale[pl.ds(block * 4 + part, 1), :]
+                    total[:, part * 128:(part + 1) * 128] * scale[pl.ds(block * 4 + part, 1), :]
                 )
 
         @pl.loop(0, 16)

time: 79.3 us -> 78.8 us (level)
  no operation moved by 1% of the time
where the time goes in v4:
time: 78.8 us; the launch traced here: 78.6 us
  Pallas kernels  77.4 us (98%)
  local copies, waits for them, and re-layouts  1.19 us (2%)
    pallas_call x1, Pallas kernels, body(): pl.pallas_call(kernel, out_shape=jax.ShapeDtypeStruct((1, 1, 64), F32), i...  77.4 us

profile of v4, /device:TPU:0, one launch (start us, length us, event | category | flops | bytes accessed | tf_op | source)
XLA Modules:
  0.0 78.6 jit_solution(2762408956722178087)
XLA Ops:
  0.0 77.4 %shard_map.55 = f32[1,1,64]{2,1,0:T(1,128)} custom-call(bf16[2,256,256]{2,1,0:T(8,128)(2,1)} %bitcast.3, bf16[1,1,32,14336]{3,2,1,0:T(8,128)(2,1)} %cot_ref.1, s32[1,256,2048]{2,1,0:T(8,128)} %bits_ref.1, s32[64,128]{1,0:T(8,128)} %bitcast.4, s32[64,128]{1,0:T(8,128)} %bitcast.5), custom_call_target="tpu_custom_call" | custom-call | tf_op jit(solution)/shard_map/pallas_call | solution.py:434
  77.4 1.2 %copy.7 = f32[1,1,64]{2,1,0:T(1,128)} copy(f32[1,1,64]{2,1,0:T(1,128)} %shard_map.55) | data formatting | bytes 512

commit v5 on v4

--- a/solution.py
+++ b/solution.py
@@ -333,6 +333,7 @@
                     table[pl.ds((2 * tile + half) * 512 + start, 8), :] = value[tile]
 
         index_copy.wait()
+        rows[1] = jnp.zeros((512, 128), F32)
 
         def dot_rows(block, held):
             span = pl.ds(pl.multiple_of(block * 512, 512), 512)
@@ -342,21 +343,27 @@
                     total[:, part * 128:(part + 1) * 128] * scale[pl.ds(block * 4 + part, 1), :]
                 )
 
-        @pl.loop(0, 16)
+        def load_rows(block, half):
+            for part in range(4):
+                for i in range(128):
+                    at = part * 128 + i
+                    rows[half, at:at + 1, :] = table[pl.ds(index[block * 4 + part, i], 1), :]
+
+        @pl.loop(0, 8)
         def _(step):
-            block = wide ^ (15 - step)
-
-            @pl.loop(0, 4)
-            def _(part):
-                base = pl.multiple_of(part * 128, 128)
-                for i in range(128):
-                    rows[0, pl.ds(base + i, 1), :] = table[pl.ds(index[block * 4 + part, i], 1), :]
-
-            dot_rows(block, rows.at[0])
-
-            @pl.when(step < 15)
+            first_block, second_block = wide ^ (15 - 2 * step), wide ^ (14 - 2 * step)
+            dot_rows(wide ^ lax.rem(16 - 2 * step, 16), rows.at[1])
+            load_rows(first_block, 0)
+
+            @pl.when(step > 0)
             def _():
-                wide_copy(15 - step).start()
+                wide_copy(16 - 2 * step).start()
+
+            dot_rows(first_block, rows.at[0])
+            load_rows(second_block, 1)
+            wide_copy(15 - 2 * step).start()
+
+        dot_rows(wide, rows.at[1])
 
     @pl.when(jnp.logical_not(real))
     def _():

time: 78.8 us -> 78.4 us (level)
  no operation moved by 1% of the time
where the time goes in v5:
time: 78.4 us; the launch traced here: 78.2 us
  Pallas kernels  77 us (98%)
  local copies, waits for them, and re-layouts  1.19 us (2%)
    pallas_call x1, Pallas kernels, body(): pl.pallas_call(kernel, out_shape=jax.ShapeDtypeStruct((1, 1, 64), F32), i...  77 us

profile of v5, /device:TPU:0, one launch (start us, length us, event | category | flops | bytes accessed | tf_op | source)
XLA Modules:
  0.0 78.2 jit_solution(5441088286796632489)
XLA Ops:
  0.0 77.0 %shard_map.55 = f32[1,1,64]{2,1,0:T(1,128)} custom-call(bf16[2,256,256]{2,1,0:T(8,128)(2,1)} %bitcast.3, bf16[1,1,32,14336]{3,2,1,0:T(8,128)(2,1)} %cot_ref.1, s32[1,256,2048]{2,1,0:T(8,128)} %bits_ref.1, s32[64,128]{1,0:T(8,128)} %bitcast.4, s32[64,128]{1,0:T(8,128)} %bitcast.5), custom_call_target="tpu_custom_call" | custom-call | tf_op jit(solution)/shard_map/pallas_call | solution.py:441
  77.0 1.2 %copy.7 = f32[1,1,64]{2,1,0:T(1,128)} copy(f32[1,1,64]{2,1,0:T(1,128)} %shard_map.55) | data formatting | bytes 512
